TPU v7x, 32 devices: a whole 2x2x4 slice. The times are simulated.
32 devices in a mesh: dp: 8 (over y, x, core), fsdp: 4 (over z).
Axes of the slice: x: 2, y: 2, z: 4, core: 2. Of those that a mesh axis runs over, the one named last changes fastest.
Arguments:
- patches: bfloat16 [16384, 1024], P(('dp', 'fsdp')), may hold values from -6 to 6
- cotangent: bfloat16 [16384, 1024], P(('dp', 'fsdp')), may hold values from -6 to 6
- ln1_gain: bfloat16 [1024], P('fsdp'), may hold values from 0.5 to 1.5
- ln1_bias: bfloat16 [1024], P('fsdp'), may hold values from -1.75 to 1.75
- w_qkv: bfloat16 [1024, 3072], P('fsdp'), may hold values from -0.1875 to 0.1875
- w_out: bfloat16 [1024, 1024], P('fsdp'), may hold values from -0.5 to 0.5
- ln2_gain: bfloat16 [1024], P('fsdp'), may hold values from 0.5 to 1.5
- ln2_bias: bfloat16 [1024], P('fsdp'), may hold values from -1.75 to 1.75
- w_fc1: bfloat16 [1024, 4096], P('fsdp'), may hold values from -0.1875 to 0.1875
- fc1_bias: bfloat16 [4096], P('fsdp'), may hold values from -3 to 3
- w_fc2: bfloat16 [4096, 1024], P('fsdp'), may hold values from -0.09375 to 0.09375
- pos_table: bfloat16 [50, 1024], P(None, 'fsdp'), may hold values from -3 to 3
- pos_index: int32 [145, 4], replicated, may hold values from 0 to 49, as said below
- pos_weight: float32 [145, 4], replicated, may hold values from 0.1 to 0.6
Outputs:
- block_out: bfloat16 [16384, 1024], P(('dp', 'fsdp'))
- input_grad: bfloat16 [16384, 1024], P(('dp', 'fsdp'))
- ln1_gain_grad: float32 [1024], P('fsdp')
- ln1_bias_grad: float32 [1024], P('fsdp')
- qkv_grad: float32 [1024, 3072], P('fsdp')
- out_proj_grad: float32 [1024, 1024], P('fsdp')
- ln2_gain_grad: float32 [1024], P('fsdp')
- ln2_bias_grad: float32 [1024], P('fsdp')
- fc1_grad: float32 [1024, 4096], P('fsdp')
- fc1_bias_grad: float32 [4096], P('fsdp')
- fc2_grad: float32 [4096, 1024], P('fsdp')
- table_grad: float32 [50, 1024], P(None, 'fsdp')
Inputs may be any that keep to these rules, and one draw needn't show every extreme that they name: `pos_index`: row 0 names row 0 four times; every other row names rows 1 + 7i + j, 2 + 7i + j, 8 + 7i + j, 9 + 7i + j for some i, j in 0 to 5.
All inputs are finite; a program needn't handle non-finite values.
Results may differ from a plain program's by a relative error of at most 0.018.
Values may be sent and summed in bfloat16 or wider, within the bound.
No kernel may reach another device: no remote copies, remote signals or barrier semaphores. Data moves between devices by JAX's collectives and lax.ppermute only.
A program may use at most 192 MiB of HBM per device.

v0:
```python
import jax
import jax.numpy as jnp
from jax import lax
from jax.sharding import PartitionSpec as P

HEADS = 16
HDIM = 64
POS = 50
HIGH_LEN = 145
highest = lax.Precision.HIGHEST


def layer_norm(hidden, gain, shift):
    centre = hidden - jnp.mean(hidden, axis=-1, keepdims=True)
    spread = jnp.mean(centre * centre, axis=-1, keepdims=True)
    return centre * lax.rsqrt(spread + 1e-06) * gain + shift


def place_rows(rows, low_flag, pos_index, pos_weight):
    offsets = jnp.arange(rows, dtype=jnp.int32)
    table_ids = jnp.arange(POS, dtype=jnp.int32)
    high_ids = jnp.arange(HIGH_LEN, dtype=jnp.int32)
    picks = (pos_index[:, :, None] == table_ids[None, None, :]).astype(jnp.float32)
    interp = jnp.sum(pos_weight[:, :, None] * picks, axis=1)
    low_valid = offsets < rows // POS * POS
    high_valid = offsets < rows // HIGH_LEN * HIGH_LEN
    low_place = (((offsets % POS)[:, None] == table_ids[None, :]) & low_valid[:, None]).astype(
        jnp.float32
    )
    high_pick = (((offsets % HIGH_LEN)[:, None] == high_ids[None, :]) & high_valid[:, None]).astype(
        jnp.float32
    )
    high_place = jnp.dot(high_pick, interp, precision=highest)
    place = jnp.where(low_flag, low_place, high_place)
    valid = jnp.where(low_flag, low_valid, high_valid)
    segment = jnp.where(
        low_flag,
        jnp.where(low_valid, offsets // POS, -1),
        jnp.where(high_valid, offsets // HIGH_LEN, -1),
    )
    return (place, valid, segment[:, None] == segment[None, :])


def split_pairs(block):
    return block.reshape(block.shape[0], HEADS // 2, 2, HDIM).transpose(1, 0, 2, 3)


def join_pairs(block):
    return block.transpose(1, 0, 2, 3).reshape(block.shape[1], HEADS * HDIM)


def masked_scores(query_pair, key_pair, mask):
    scores = jnp.einsum(
        "qhd,khd->hqk", query_pair, key_pair, preferred_element_type=jnp.float32
    ) * HDIM ** (-0.5)
    return jnp.where(mask[None], scores, -1e30)


def forward(patches, params, place, mask):
    gain_one, bias_one, w_qkv, w_out, gain_two, bias_two, w_fc1, fc1_bias, w_fc2, pos_table = params
    width = w_out.shape[0]
    hidden_in = patches.astype(jnp.float32) + jnp.dot(
        place, pos_table.astype(jnp.float32), precision=highest
    )
    normed_one = layer_norm(
        hidden_in, gain_one.astype(jnp.float32), bias_one.astype(jnp.float32)
    ).astype(jnp.bfloat16)
    projected = jnp.dot(normed_one, w_qkv, preferred_element_type=jnp.float32).astype(jnp.bfloat16)
    queries = split_pairs(projected[:, :width])
    keys = split_pairs(projected[:, width : 2 * width])
    values = split_pairs(projected[:, 2 * width :])

    def attend(items):
        query_pair, key_pair, value_pair = items
        scores = masked_scores(query_pair, key_pair, mask)
        peak = jnp.max(scores, axis=-1, keepdims=True)
        expo = jnp.exp(scores - peak)
        total = jnp.sum(expo, axis=-1, keepdims=True)
        probs = (expo / total).astype(jnp.bfloat16)
        mixed = jnp.einsum("hqk,khd->qhd", probs, value_pair, preferred_element_type=jnp.float32)
        return (mixed.astype(jnp.bfloat16), (peak + jnp.log(total))[..., 0])

    attended, log_norm = lax.map(attend, (queries, keys, values))
    attn_rows = join_pairs(attended)
    hidden_mid = hidden_in + jnp.dot(attn_rows, w_out, preferred_element_type=jnp.float32)
    normed_two = layer_norm(
        hidden_mid, gain_two.astype(jnp.float32), bias_two.astype(jnp.float32)
    ).astype(jnp.bfloat16)
    pre_act = jnp.dot(normed_two, w_fc1, preferred_element_type=jnp.float32) + fc1_bias.astype(
        jnp.float32
    )
    activated = jax.nn.gelu(pre_act, approximate=False).astype(jnp.bfloat16)
    branch_out = jnp.dot(activated, w_fc2, preferred_element_type=jnp.float32)
    return (
        hidden_in,
        normed_one,
        projected,
        log_norm,
        attn_rows,
        hidden_mid,
        normed_two,
        pre_act,
        activated,
        branch_out,
    )


def backward(kept, params, place, mask, grad_out):
    gain_one, bias_one, w_qkv, w_out, gain_two, bias_two, w_fc1, fc1_bias, w_fc2, pos_table = params
    (
        hidden_in,
        normed_one,
        projected,
        log_norm,
        attn_rows,
        hidden_mid,
        normed_two,
        pre_act,
        activated,
        branch_out,
    ) = kept
    width = w_out.shape[0]
    grad_fc2 = jnp.einsum("rf,rd->fd", activated, grad_out, preferred_element_type=jnp.float32)
    grad_act = jnp.einsum("rd,fd->rf", grad_out, w_fc2, preferred_element_type=jnp.float32)
    _, pull_gelu = jax.vjp(lambda inner: jax.nn.gelu(inner, approximate=False), pre_act)
    grad_pre = pull_gelu(grad_act)[0].astype(jnp.bfloat16)
    grad_fc1_bias = jnp.sum(grad_pre.astype(jnp.float32), axis=0)
    grad_fc1 = jnp.einsum("rd,rf->df", normed_two, grad_pre, preferred_element_type=jnp.float32)
    grad_norm_two = jnp.einsum("rf,df->rd", grad_pre, w_fc1, preferred_element_type=jnp.float32)
    _, pull_two = jax.vjp(
        layer_norm, hidden_mid, gain_two.astype(jnp.float32), bias_two.astype(jnp.float32)
    )
    back_mid, grad_gain_two, grad_bias_two = pull_two(grad_norm_two)
    grad_mid = grad_out.astype(jnp.float32) + back_mid
    grad_branch = grad_mid.astype(jnp.bfloat16)
    grad_wout = jnp.einsum("rd,re->de", attn_rows, grad_branch, preferred_element_type=jnp.float32)
    grad_attn = jnp.einsum(
        "re,de->rd", grad_branch, w_out, preferred_element_type=jnp.float32
    ).astype(jnp.bfloat16)
    queries = split_pairs(projected[:, :width])
    keys = split_pairs(projected[:, width : 2 * width])
    values = split_pairs(projected[:, 2 * width :])
    grad_pairs = split_pairs(grad_attn)

    def attend_back(items):
        query_pair, key_pair, value_pair, grad_pair, log_pair = items
        scores = masked_scores(query_pair, key_pair, mask)
        probs = jnp.exp(scores - log_pair[..., None])
        probs_low = probs.astype(jnp.bfloat16)
        grad_probs = jnp.einsum(
            "qhd,khd->hqk", grad_pair, value_pair, preferred_element_type=jnp.float32
        )
        centre = jnp.sum(probs * grad_probs, axis=-1, keepdims=True)
        grad_scores = (probs * (grad_probs - centre)).astype(jnp.bfloat16)
        grad_query = jnp.einsum(
            "hqk,khd->qhd", grad_scores, key_pair, preferred_element_type=jnp.float32
        ) * HDIM ** (-0.5)
        grad_key = jnp.einsum(
            "hqk,qhd->khd", grad_scores, query_pair, preferred_element_type=jnp.float32
        ) * HDIM ** (-0.5)
        grad_value = jnp.einsum(
            "hqk,qhd->khd", probs_low, grad_pair, preferred_element_type=jnp.float32
        )
        return (grad_query, grad_key, grad_value)

    grad_query, grad_key, grad_value = lax.map(
        attend_back, (queries, keys, values, grad_pairs, log_norm)
    )
    grad_proj = jnp.concatenate(
        [join_pairs(grad_query), join_pairs(grad_key), join_pairs(grad_value)], axis=1
    ).astype(jnp.bfloat16)
    grad_qkv = jnp.einsum("rd,re->de", normed_one, grad_proj, preferred_element_type=jnp.float32)
    grad_norm_one = jnp.einsum("re,de->rd", grad_proj, w_qkv, preferred_element_type=jnp.float32)
    _, pull_one = jax.vjp(
        layer_norm, hidden_in, gain_one.astype(jnp.float32), bias_one.astype(jnp.float32)
    )
    back_in, grad_gain_one, grad_bias_one = pull_one(grad_norm_one)
    grad_in = grad_mid + back_in
    grad_table = jnp.dot(place.T, grad_in, precision=highest)
    grads = (
        grad_gain_one,
        grad_bias_one,
        grad_qkv,
        grad_wout,
        grad_gain_two,
        grad_bias_two,
        grad_fc1,
        grad_fc1_bias,
        grad_fc2,
        grad_table,
    )
    return (grad_in.astype(jnp.bfloat16), grads)


def per_device(
    patches,
    cotangent,
    ln1_gain,
    ln1_bias,
    w_qkv,
    w_out,
    ln2_gain,
    ln2_bias,
    w_fc1,
    fc1_bias,
    w_fc2,
    pos_table,
    pos_index,
    pos_weight,
):
    n_data = lax.axis_size("dp")
    low_flag = lax.axis_index("dp") < n_data * 7 // 16
    rows = patches.shape[0]
    place, valid, mask = place_rows(rows, low_flag, pos_index, pos_weight)
    gathered = (
        lax.all_gather(ln1_gain, "fsdp", axis=0, tiled=True),
        lax.all_gather(ln1_bias, "fsdp", axis=0, tiled=True),
        lax.all_gather(w_qkv, "fsdp", axis=0, tiled=True),
        lax.all_gather(w_out, "fsdp", axis=0, tiled=True),
        lax.all_gather(ln2_gain, "fsdp", axis=0, tiled=True),
        lax.all_gather(ln2_bias, "fsdp", axis=0, tiled=True),
        lax.all_gather(w_fc1, "fsdp", axis=0, tiled=True),
        lax.all_gather(fc1_bias, "fsdp", axis=0, tiled=True),
        lax.all_gather(w_fc2, "fsdp", axis=0, tiled=True),
        lax.all_gather(pos_table, "fsdp", axis=1, tiled=True),
    )
    kept = forward(patches, gathered, place, mask)
    block_out = jnp.where(valid[:, None], kept[5] + kept[9], 0.0).astype(jnp.bfloat16)
    regathered = (
        lax.all_gather(ln1_gain, "fsdp", axis=0, tiled=True),
        lax.all_gather(ln1_bias, "fsdp", axis=0, tiled=True),
        lax.all_gather(w_qkv, "fsdp", axis=0, tiled=True),
        lax.all_gather(w_out, "fsdp", axis=0, tiled=True),
        lax.all_gather(ln2_gain, "fsdp", axis=0, tiled=True),
        lax.all_gather(ln2_bias, "fsdp", axis=0, tiled=True),
        lax.all_gather(w_fc1, "fsdp", axis=0, tiled=True),
        lax.all_gather(fc1_bias, "fsdp", axis=0, tiled=True),
        lax.all_gather(w_fc2, "fsdp", axis=0, tiled=True),
        lax.all_gather(pos_table, "fsdp", axis=1, tiled=True),
    )
    rekept = forward(patches, regathered, place, mask)
    grad_out = jnp.where(valid[:, None], cotangent, jnp.zeros_like(cotangent))
    input_grad, grads = backward(rekept, regathered, place, mask, grad_out)
    shares = (
        lax.psum_scatter(
            grads[0].astype(jnp.bfloat16), "fsdp", scatter_dimension=0, tiled=True
        ).astype(jnp.float32),
        lax.psum_scatter(
            grads[1].astype(jnp.bfloat16), "fsdp", scatter_dimension=0, tiled=True
        ).astype(jnp.float32),
        lax.psum_scatter(
            grads[2].astype(jnp.bfloat16), "fsdp", scatter_dimension=0, tiled=True
        ).astype(jnp.float32),
        lax.psum_scatter(
            grads[3].astype(jnp.bfloat16), "fsdp", scatter_dimension=0, tiled=True
        ).astype(jnp.float32),
        lax.psum_scatter(
            grads[4].astype(jnp.bfloat16), "fsdp", scatter_dimension=0, tiled=True
        ).astype(jnp.float32),
        lax.psum_scatter(
            grads[5].astype(jnp.bfloat16), "fsdp", scatter_dimension=0, tiled=True
        ).astype(jnp.float32),
        lax.psum_scatter(
            grads[6].astype(jnp.bfloat16), "fsdp", scatter_dimension=0, tiled=True
        ).astype(jnp.float32),
        lax.psum_scatter(
            grads[7].astype(jnp.bfloat16), "fsdp", scatter_dimension=0, tiled=True
        ).astype(jnp.float32),
        lax.psum_scatter(
            grads[8].astype(jnp.bfloat16), "fsdp", scatter_dimension=0, tiled=True
        ).astype(jnp.float32),
        lax.psum_scatter(
            grads[9].astype(jnp.bfloat16), "fsdp", scatter_dimension=1, tiled=True
        ).astype(jnp.float32),
    )
    totals = (
        lax.psum(shares[0].astype(jnp.bfloat16), "dp").astype(jnp.float32),
        lax.psum(shares[1].astype(jnp.bfloat16), "dp").astype(jnp.float32),
        lax.psum(shares[2].astype(jnp.bfloat16), "dp").astype(jnp.float32),
        lax.psum(shares[3].astype(jnp.bfloat16), "dp").astype(jnp.float32),
        lax.psum(shares[4].astype(jnp.bfloat16), "dp").astype(jnp.float32),
        lax.psum(shares[5].astype(jnp.bfloat16), "dp").astype(jnp.float32),
        lax.psum(shares[6].astype(jnp.bfloat16), "dp").astype(jnp.float32),
        lax.psum(shares[7].astype(jnp.bfloat16), "dp").astype(jnp.float32),
        lax.psum(shares[8].astype(jnp.bfloat16), "dp").astype(jnp.float32),
        lax.psum(shares[9].astype(jnp.bfloat16), "dp").astype(jnp.float32),
    )
    return (
        block_out,
        input_grad,
        totals[0],
        totals[1],
        totals[2],
        totals[3],
        totals[4],
        totals[5],
        totals[6],
        totals[7],
        totals[8],
        totals[9],
    )


def solution(mesh):
    return jax.shard_map(
        per_device,
        mesh=mesh,
        in_specs=(
            P(("dp", "fsdp"), None),
            P(("dp", "fsdp"), None),
            P("fsdp"),
            P("fsdp"),
            P("fsdp", None),
            P("fsdp", None),
            P("fsdp"),
            P("fsdp"),
            P("fsdp", None),
            P("fsdp"),
            P("fsdp", None),
            P(None, "fsdp"),
            P(),
            P(),
        ),
        out_specs=(
            P(("dp", "fsdp"), None),
            P(("dp", "fsdp"), None),
            P("fsdp"),
            P("fsdp"),
            P("fsdp", None),
            P("fsdp", None),
            P("fsdp"),
            P("fsdp"),
            P("fsdp", None),
            P("fsdp"),
            P("fsdp", None),
            P(None, "fsdp"),
        ),
        check_vma=False,
    )
```

profile of v0, /device:TPU:0, one launch (start us, length us, event | category | flops | bytes accessed | tf_op | source)
XLA Modules:
  0.0 1141.8 jit_solution(14354497924452631395)
XLA Ops:
  10.2 15.1 %all_gather.40 = bf16[50,1024]{1,0:T(8,128)(2,1)S(1)} all-gather(bf16[50,256]{1,0:T(8,128)(2,1)S(1)} %copy-done.16), channel_id=1, replica_groups=mesh['dp'=8,'fsdp'=4] {'fsdp'}, dimensions={1}, use_global_device_ids=true | all-gather | bytes 128000 | tf_op jit(solution)/shard_map/all_gather | solution.py:225
  27.7 12.1 %all-gather = bf16[4,1,256]{2,1,0:T(2,128)(2,1)S(1)} all-gather(bf16[1,1,256]{2,1,0:T(2,128)(2,1)S(1)} %reshape.257), channel_id=1, replica_groups=mesh['dp'=8,'fsdp'=4] {'fsdp'}, dimensions={0}, use_global_device_ids=true | all-gather | bytes 2560 | tf_op jit(solution)/shard_map/all_gather | solution.py:216
  39.8 8.5 all-gather.1
  48.3 14.1 %all-gather.2 = bf16[4,1,256]{2,1,0:T(2,128)(2,1)S(1)} all-gather(bf16[1,1,256]{2,1,0:T(2,128)(2,1)S(1)} %reshape.261), channel_id=1, replica_groups=mesh['dp'=8,'fsdp'=4] {'fsdp'}, dimensions={0}, use_global_device_ids=true | all-gather | bytes 2560 | tf_op jit(solution)/shard_map/all_gather | solution.py:220
  62.4 17.2 %all_gather.48 = bf16[4096]{0:T(1024)(128)(2,1)S(1)} all-gather(bf16[1024]{0:T(1024)(128)(2,1)S(1)} %copy-done.22), channel_id=1, replica_groups=mesh['dp'=8,'fsdp'=4] {'fsdp'}, dimensions={0}, use_global_device_ids=true | all-gather | bytes 10240 | tf_op jit(solution)/shard_map/all_gather | solution.py:223
  79.7 8.2 all-gather.3
  87.9 40.0 %all-gather.9.cloned.1.call-done = bf16[1024,3072]{1,0:T(8,128)(2,1)} async-done(((bf16[256,3072]{1,0:T(8,128)(2,1)}), bf16[1024,3072]{1,0:T(8,128)(2,1)}) %all-gather.9.cloned.1.call-update) | async-done | bytes 6291472 | tf_op jit(solution)/shard_map/all_gather | solution.py:218
  128.0 6.6 convolution_convert_fusion.5
  142.4 36.8 %while.40 = (s32[]{:T(128)}, bf16[8,512,2,64]{1,3,2,0:T(8,128)(2,1)}, f32[8,2,512]{2,1,0:T(2,128)S(1)}, bf16[8,512,2,64]{1,3,2,0:T(8,128)(2,1)}, bf16[8,512,2,64...) while((s32[]{:T(128)}, ...), condition=%wide.region_12.13_spmd.clone, body=%wide.region_9.12_spmd.clone.sunk | while | flops 140835840 | bytes 7901273 | solution.py:83
  144.7 2.3 fusion.277
  149.3 2.3 fusion.277
  153.9 2.3 fusion.277
  158.5 2.3 fusion.277
  163.1 2.3 fusion.277
  167.7 2.3 fusion.277
  172.3 2.3 fusion.277
  179.2 4.0 fusion.218
  184.9 138.7 %all-gather.13.cloned.1.call-done = bf16[1024,4096]{1,0:T(8,128)(2,1)} async-done(((bf16[256,4096]{1,0:T(8,128)(2,1)}), bf16[1024,4096]{1,0:T(8,128)(2,1)}) %all-gather.13.cloned.1.call-update) | async-done | bytes 8388624 | tf_op jit(solution)/shard_map/all_gather | solution.py:222
  323.6 28.0 %fusion.98 = (f32[512,4096]{1,0:T(8,128)}, f32[512,4096]{1,0:T(8,128)}) fusion(f32[4096]{0:T(1024)S(1)} %convert_element_type.184, bf16[1024,4096]{1,0:T(8,128)(2,1)} %all-gather.13.cloned.1.call-done, f32[512,1024]{1,0:T(8,128)} %copy-done.2, f32[512]{0:T(512)S(1)} %fusion.171, f32[512]{0:T(512)S(1)} %broadcast_multiply_fusion, f32[1024]{0:T(1024)S(1)} %bitcast.216, ...), kind=kOutput, calls=%fused_computation.96 | convolution fusion | flops 4429709312 | bytes 27291648 | tf_op jit(solution)/shard_map/dot_general | solution.py:89
  351.6 121.2 %all-gather.15.cloned.1.call-done = bf16[4096,1024]{1,0:T(8,128)(2,1)} async-done(((bf16[1024,1024]{1,0:T(8,128)(2,1)}), bf16[4096,1024]{1,0:T(8,128)(2,1)}) %all-gather.15.cloned.1.call-update) | async-done | bytes 8388624 | tf_op jit(solution)/shard_map/all_gather | solution.py:224
  472.8 15.7 %fusion.219 = (bf16[4096]{0:T(1024)(128)(2,1)}, bf16[512,4096]{1,0:T(8,128)(2,1)}) fusion(f32[512,4096]{1,0:T(8,128)} %get-tuple-element.283, bf16[4096,1024]{1,0:T(8,128)(2,1)} %all-gather.15.cloned.1.call-done, bf16[512,1024]{1,0:T(8,128)(2,1)S(1)} %copy-done.5, pred[512]{0:T(512)(128)(4,1)S(1)} %broadcast_select_fusion.1, ...), kind=kOutput, calls=%fused_computation.279 | convolution fusion | flops 4329041920 | bytes 30433792 | tf_op jit(solution)/shard_map/rd,fd->rf/dot_general | solution.py:124
  488.6 9.3 multiply_reduce_fusion.1
  501.3 3.8 convolution_convert_fusion.6
  505.2 4.2 convolution_convert_fusion.7
  511.1 72.4 %while.41 = (s32[]{:T(128)}, bf16[8,512,2,64]{1,3,2,0:T(8,128)(2,1)}, bf16[8,512,2,64]{1,3,2,0:T(8,128)(2,1)}, bf16[8,512,2,64]{1,3,2,0:T(8,128)(2,1)}, bf16[8,5...) while((s32[]{:T(128)}, ...), condition=%wide.region_19.20_spmd.clone, body=%wide.region_17.19_spmd.clone.sunk | while | flops 340655104 | bytes 17984624 | solution.py:166
  583.5 8.3 convolution_convert_fusion.4
  593.0 15.1 %convolution_convert_fusion.2 = bf16[4096,1024]{1,0:T(8,128)(2,1)} fusion(f32[512,4096]{1,0:T(8,128)} %get-tuple-element.283, f32[512,4096]{1,0:T(8,128)} %get-tuple-element.284, f32[4096]{0:T(1024)S(1)} %convert_element_type.184, bf16[512,1024]{1,0:T(8,128)(2,1)S(1)} %copy-done.6, pred[512]{0:T(512)(128)(4,1)S(1)} %broadcast_select_fusion.1), kind=kOutput, calls=%fused_computation.127 | convolution fusion | flops 4308074496 | bytes 26231296 | tf_op jit(solution)/shard_map/rf,rd->fd/dot_general | solution.py:123
  608.2 10.8 convolution_convert_fusion.3
  622.6 40.7 %while.39 = (s32[]{:T(128)}, bf16[8,512,2,64]{1,3,2,0:T(8,128)(2,1)}, bf16[8,512,2,64]{1,3,2,0:T(8,128)(2,1)}, bf16[8,512,2,64]{1,3,2,0:T(8,128)(2,1)}, bf16[8,5...) while((s32[]{:T(128)}, bf16[8,512,2,64]{1,3,2,0:T(8,128)(2,1)}, ...), condition=%wide.region_6.7_spmd.clone, body=%wide.region_3.6_spmd.clone.sunk | while | flops 206374912 | bytes 1586253 | solution.py:83
  624.8 2.9 fusion.273
  629.9 2.9 fusion.273
  635.0 2.9 fusion.273
  640.0 2.9 fusion.273
  645.1 2.9 fusion.273
  650.2 2.9 fusion.273
  655.3 2.9 fusion.273
  660.4 2.9 fusion.273
  663.3 3.5 fusion.217
  668.4 7.3 multiply_reduce_fusion.2
  681.0 19.9 %reduce-scatter.6.cloned.1.call-done = bf16[256,3072]{1,0:T(8,128)(2,1)} async-done(((bf16[1024,3072]{1,0:T(8,128)(2,1)}), bf16[256,3072]{1,0:T(8,128)(2,1)}) %reduce-scatter.6.cloned.1.call-update) | async-done | bytes 1572880 | tf_op jit(solution)/shard_map/reduce_scatter | solution.py:251
  700.9 147.5 %reduce-scatter.12.cloned.1.call-done = bf16[1024,1024]{1,0:T(8,128)(2,1)} async-done(((bf16[4096,1024]{1,0:T(8,128)(2,1)}), bf16[1024,1024]{1,0:T(8,128)(2,1)}) %reduce-scatter.12.cloned.1.call-update) | async-done | bytes 2097168 | tf_op jit(solution)/shard_map/reduce_scatter | solution.py:269
  848.5 147.6 %reduce-scatter.10.cloned.1.call-done = bf16[256,4096]{1,0:T(8,128)(2,1)} async-done(((bf16[1024,4096]{1,0:T(8,128)(2,1)}), bf16[256,4096]{1,0:T(8,128)(2,1)}) %reduce-scatter.10.cloned.1.call-update) | async-done | bytes 2097168 | tf_op jit(solution)/shard_map/reduce_scatter | solution.py:263
  996.1 32.4 %select_convert_fusion = bf16[512,1024]{1,0:T(8,128)(2,1)} fusion(f32[512,1024]{1,0:T(8,128)S(1)} %copy-done.9, bf16[4096,1024]{1,0:T(8,128)(2,1)} %all-gather.15.cloned.1.call-done, bf16[1024,4096]{1,0:T(8,128)(2,1)} %all-gather.13.cloned.1.call-done, f32[4096]{0:T(1024)S(1)} %convert_element_type.184, f32[1024]{0:T(1024)S(1)} %bitcast.218, ...), kind=kOutput, calls=%fused_computation.176 | convolution fusion | flops 8732540928 | bytes 19952128 | tf_op jit(solution)/shard_map/dot_general | solution.py:93
  1028.6 18.1 %all-reduce.7 = (bf16[1024]{0:T(1024)(128)(2,1)S(1)}, bf16[1024]{0:T(1024)(128)(2,1)S(1)}, bf16[1024]{0:T(1024)(128)(2,1)S(1)}, bf16[1024]{0:T(1024)(128)(2,1)S(1)}, bf16[4096]{0:T(1024)(128)(2,1)S(1)}) all-reduce(bf16[1024]{0:T(1024)(128)(2,1)S(1)} %get-tuple-element.199, ...), channel_id=2, replica_groups=mesh['dp'=8,'fsdp'=4] {'fsdp'}, use_global_device_ids=true, to_apply=%region_23.24.clone | all-reduce | flops 8192 | bytes 32768
  1047.0 23.9 %all-reduce.5 = (bf16[256]{0:T(256)(128)(2,1)S(1)}, bf16[256]{0:T(256)(128)(2,1)S(1)}, bf16[256]{0:T(256)(128)(2,1)S(1)}, bf16[256]{0:T(256)(128)(2,1)S(1)}, bf1...) all-reduce(bf16[256]{0:T(256)(128)(2,1)S(1)} %dynamic-slice.1, ...), channel_id=1, replica_groups=mesh['dp'=8,'fsdp'=4] {'dp'}, use_global_device_ids=true, to_apply=%region_24.25 | all-reduce | flops 14848 | bytes 59392 | tf_op jit(solution)/shard_map/psum | solution.py:277
  1074.4 50.6 %all-reduce.10.cloned.1.call-done = (bf16[256,3072]{1,0:T(8,128)(2,1)}, bf16[256,1024]{1,0:T(8,128)(2,1)}, bf16[256,4096]{1,0:T(8,128)(2,1)}, bf16[1024,1024]{1,0:T(8,128)(2,1)}) async-done(((bf16[256,3072]{1,0:T(8,128)(2,1)}, bf16[256,1024]{1,0:T(8,128)(2,1)}, bf16[256,4096]{1,0:T(8,128)(2,1)}, bf16[1024,1024]{1,0:T(8,128)(2,1)}), (bf16[256,3072]{1,0:T(8,128)(2,1)}, bf16[256,1024]{1,0:T(8,128)(2,1)}, ...) | async-done | bytes 6291472 | tf_op jit(solution)/shard_map/psum | solution.py:279
  1124.9 4.2 convert_element_type.206
  1129.2 2.5 convert_element_type.210
  (259 shorter events, 147.0 us)
Async XLA Ops:
  7.2 3.0 copy-start.16
  7.2 18.2 %copy-start.21 = (s32[145,4]{0,1:T(4,128)S(1)}, s32[145,4]{0,1:T(4,128)}, u32[]{:S(2)}) copy-start(s32[145,4]{0,1:T(4,128)} %param.32) | copy-start | bytes 6964
  7.2 18.1 %copy-start.20 = (f32[145,4]{0,1:T(4,128)S(1)}, f32[145,4]{0,1:T(4,128)}, u32[]{:S(2)}) copy-start(f32[145,4]{0,1:T(4,128)} %param.33) | copy-start | bytes 6964
  7.2 18.8 %copy-start.11 = (bf16[512,1024]{1,0:T(8,128)(2,1)S(1)}, bf16[512,1024]{1,0:T(8,128)(2,1)}, u32[]{:S(2)}) copy-start(bf16[512,1024]{1,0:T(8,128)(2,1)} %param.20) | copy-start | bytes 3145732
  7.2 120.7 %all-gather.9.cloned.1.call-start = ((), (), s32[]{:S(2)}) async-start(), calls=%async_computation.5 | async-start | bytes 7864320 | tf_op jit(solution)/shard_map/all_gather | solution.py:218
  8.0 171.3 %all-gather.11.cloned.1.call-start = ((), (), s32[]{:S(2)}) async-start(), calls=%async_computation.6 | async-start | bytes 2621440 | tf_op jit(solution)/shard_map/all_gather | solution.py:219
  8.7 314.9 %all-gather.13.cloned.1.call-start = ((), (), s32[]{:S(2)}) async-start(), calls=%async_computation.7 | async-start | bytes 10485760 | tf_op jit(solution)/shard_map/all_gather | solution.py:222
  9.4 18.2 %copy-start.27 = (bf16[256]{0:T(256)(128)(2,1)S(1)}, bf16[256]{0:T(256)(128)(2,1)}, u32[]{:S(2)}) copy-start(bf16[256]{0:T(256)(128)(2,1)} %param.22) | copy-start | bytes 1540
  9.4 30.3 %copy-start.28 = (bf16[256]{0:T(256)(128)(2,1)S(1)}, bf16[256]{0:T(256)(128)(2,1)}, u32[]{:S(2)}) copy-start(bf16[256]{0:T(256)(128)(2,1)} %param.23) | copy-start | bytes 1540
  9.5 38.8 %copy-start.29 = (bf16[256]{0:T(256)(128)(2,1)S(1)}, bf16[256]{0:T(256)(128)(2,1)}, u32[]{:S(2)}) copy-start(bf16[256]{0:T(256)(128)(2,1)} %param.26) | copy-start | bytes 1540
  9.5 53.0 %copy-start.22 = (bf16[1024]{0:T(1024)(128)(2,1)S(1)}, bf16[1024]{0:T(1024)(128)(2,1)}, u32[]{:S(2)}) copy-start(bf16[1024]{0:T(1024)(128)(2,1)} %param.29) | copy-start | bytes 6148
  9.5 70.2 %copy-start.30 = (bf16[256]{0:T(256)(128)(2,1)S(1)}, bf16[256]{0:T(256)(128)(2,1)}, u32[]{:S(2)}) copy-start(bf16[256]{0:T(256)(128)(2,1)} %param.27) | copy-start | bytes 1540
  9.5 463.3 %all-gather.15.cloned.1.call-start = ((), (), s32[]{:S(2)}) async-start(), calls=%async_computation.8 | async-start | bytes 10485760 | tf_op jit(solution)/shard_map/all_gather | solution.py:224
  10.1 670.9 %reduce-scatter.8.cloned.1.call-start = ((), (), s32[]{:S(2)}) async-start(), calls=%async_computation.10 | async-start | bytes 2621440 | tf_op jit(solution)/shard_map/reduce_scatter | solution.py:254
  26.0 108.6 %copy-start.14 = (f32[512,50]{0,1:T(8,128)}, f32[512,50]{0,1:T(8,128)S(1)}, u32[]{:S(2)}) copy-start(f32[512,50]{0,1:T(8,128)S(1)} %convolution_select_fusion) | copy-start | bytes 307204
  27.6 34.8 %copy-start.17 = (f32[512]{0:T(512)}, f32[512]{0:T(512)S(1)}, u32[]{:S(2)}) copy-start(f32[512]{0:T(512)S(1)} %multiply_reduce_fusion.7) | copy-start | bytes 6148
  179.2 5.7 copy-start.4
  183.2 1.3 copy-start.2
  323.6 149.3 %copy-start.5 = (bf16[512,1024]{1,0:T(8,128)(2,1)S(1)}, bf16[512,1024]{1,0:T(8,128)(2,1)}, u32[]{:S(2)}) copy-start(bf16[512,1024]{1,0:T(8,128)(2,1)} %param.21) | copy-start | bytes 3145732
  472.8 15.7 %copy-start.3 = (f32[512,1024]{1,0:T(8,128)S(1)}, f32[512,1024]{1,0:T(8,128)}, u32[]{:S(2)}) copy-start(f32[512,1024]{1,0:T(8,128)} %copy-done.2) | copy-start | bytes 6291460
  498.6 1.3 copy-start
  500.3 1.0 copy-start.12
  505.1 195.8 %reduce-scatter.6.cloned.1.call-start = ((), (), s32[]{:S(2)}) async-start(), calls=%async_computation.9 | async-start | bytes 7864320 | tf_op jit(solution)/shard_map/reduce_scatter | solution.py:251
  591.8 1.2 copy-start.6
  591.8 256.6 %reduce-scatter.12.cloned.1.call-start = ((), (), s32[]{:S(2)}) async-start(), calls=%async_computation.12 | async-start | bytes 10485760 | tf_op jit(solution)/shard_map/reduce_scatter | solution.py:269
  608.1 388.0 %reduce-scatter.10.cloned.1.call-start = ((), (), s32[]{:S(2)}) async-start(), calls=%async_computation.11 | async-start | bytes 10485760 | tf_op jit(solution)/shard_map/reduce_scatter | solution.py:263
  619.0 0.7 copy-start.31
  619.0 428.0 %reduce-scatter.14.cloned.1.call-start = ((), (), s32[]{:S(2)}) async-start(), calls=%async_computation.13 | async-start | bytes 143360 | tf_op jit(solution)/shard_map/reduce_scatter | solution.py:272
  663.3 5.2 copy-start.25
  663.3 5.2 copy-start.26
  666.8 1.3 copy-start.8
  668.4 7.3 copy-start.18
  675.7 1.6 copy-start.1
  677.3 1.5 copy-start.15
  678.9 317.2 %copy-start.9 = (f32[512,1024]{1,0:T(8,128)S(1)}, f32[512,1024]{1,0:T(8,128)}, u32[]{:S(2)}) copy-start(f32[512,1024]{1,0:T(8,128)} %copy-done.8) | copy-start | bytes 6291460
  680.9 444.0 %all-reduce.10.cloned.1.call-start = ((), (), s32[]{:S(2)}) async-start(), calls=%async_computation.14 | async-start | bytes 12582912 | tf_op jit(solution)/shard_map/psum | solution.py:279
  996.1 32.5 %copy-start.19 = (bf16[4096]{0:T(1024)(128)(2,1)S(1)}, bf16[4096]{0:T(1024)(128)(2,1)}, u32[]{:S(2)}) copy-start(bf16[4096]{0:T(1024)(128)(2,1)} %get-tuple-element.287) | copy-start | bytes 24580
  996.1 32.5 %copy-start.23 = (bf16[1024]{0:T(1024)(128)(2,1)S(1)}, bf16[1024]{0:T(1024)(128)(2,1)}, u32[]{:S(2)}) copy-start(bf16[1024]{0:T(1024)(128)(2,1)} %get-tuple-element.197) | copy-start | bytes 6148
  996.1 32.5 %copy-start.24 = (bf16[1024]{0:T(1024)(128)(2,1)S(1)}, bf16[1024]{0:T(1024)(128)(2,1)}, u32[]{:S(2)}) copy-start(bf16[1024]{0:T(1024)(128)(2,1)} %get-tuple-element.201) | copy-start | bytes 6148
  1124.9 4.3 copy-start.7
  1129.2 2.5 copy-start.10
  1129.2 4.5 copy-start.13
Sparse Core Ops, SparseCore 0:
  9.6 118.3 all-gather.8
  129.5 43.9 all-gather.10
  175.0 148.4 all-gather.12
  325.0 147.7 all-gather.14
  505.3 41.7 reduce-scatter.7
  591.9 108.9 reduce-scatter.5
  703.3 145.1 reduce-scatter.11
  850.8 145.2 reduce-scatter.9
  998.9 20.0 reduce-scatter.13
  1022.4 102.4 all-reduce.9
where the time goes:
time: 1150 us; the launch traced here: 1140 us
  waiting for transfers between devices  668 us (58%)
  matrix products  288 us (25%)
  blocking collectives  117 us (10%)
  other arithmetic  31.7 us (3%)
  local copies, waits for them, and re-layouts  18.6 us (2%)
  between operations  16.1 us (1%)
    reduce_scatter x1, waiting for transfers between devices, per_device(): lax.psum_scatter(grads[6].astype(jnp.bfloat16), 'fsdp', scatter_dimension...  148 us
    reduce_scatter x1, waiting for transfers between devices, per_device(): lax.psum_scatter(grads[8].astype(jnp.bfloat16), 'fsdp', scatter_dimension...  148 us
    all_gather x1, waiting for transfers between devices, per_device(): lax.all_gather(w_fc1, 'fsdp', axis=0, tiled=True)  139 us
    all_gather x1, waiting for transfers between devices, per_device(): lax.all_gather(w_fc2, 'fsdp', axis=0, tiled=True)  121 us
    psum x1, waiting for transfers between devices, per_device(): lax.psum(shares[2].astype(jnp.bfloat16), 'dp').astype(jnp.float32)  50.6 us
    dot_general x16, matrix products, attend(): jnp.einsum('hqk,khd->qhd', probs, value_pair, preferred_element_type=jnp....  41.9 us
    all_gather x1, waiting for transfers between devices, per_device(): lax.all_gather(w_qkv, 'fsdp', axis=0, tiled=True)  40 us
    dot_general x1, matrix products, forward(): branch_out = jnp.dot(activated, w_fc2, preferred_element_type=jnp.float32)  32.4 us
  transfers between devices with their start and end apart: 10, of which 7 were waited for; matrix products, arithmetic and copies ran while one was open for 26% of the time, Pallas kernels for 0%

commit v1 on v0

--- a/solution.py
+++ b/solution.py
@@ -8,6 +8,24 @@
 POS = 50
 HIGH_LEN = 145
 highest = lax.Precision.HIGHEST
+
+
+def collect(shard, axis, dim):
+    ways, here, turn = (lax.axis_size(axis), lax.axis_index(axis), shard.shape[dim])
+    shape = [n * ways if d == dim else n for d, n in enumerate(shard.shape)]
+    full = lax.dynamic_update_slice_in_dim(
+        jnp.zeros(shape, shard.dtype), shard, here * turn, axis=dim
+    )
+    going_up = going_down = shard
+    for far in range(1, ways // 2 + 1):
+        going_up = lax.ppermute(going_up, axis, [(d, (d + 1) % ways) for d in range(ways)])
+        full = lax.dynamic_update_slice_in_dim(full, going_up, (here - far) % ways * turn, axis=dim)
+        if 2 * far < ways:
+            going_down = lax.ppermute(going_down, axis, [(d, (d - 1) % ways) for d in range(ways)])
+            full = lax.dynamic_update_slice_in_dim(
+                full, going_down, (here + far) % ways * turn, axis=dim
+            )
+    return full
 
 
 def layer_norm(hidden, gain, shift):
@@ -221,7 +239,7 @@
         lax.all_gather(ln2_bias, "fsdp", axis=0, tiled=True),
         lax.all_gather(w_fc1, "fsdp", axis=0, tiled=True),
         lax.all_gather(fc1_bias, "fsdp", axis=0, tiled=True),
-        lax.all_gather(w_fc2, "fsdp", axis=0, tiled=True),
+        collect(w_fc2, "fsdp", 0),
         lax.all_gather(pos_table, "fsdp", axis=1, tiled=True),
     )
     kept = forward(patches, gathered, place, mask)

time: 1150 us -> 1270 us (1.10)
  waiting for transfers between devices: 668 us -> 772 us
  local copies, waits for them, and re-layouts: 18.6 us -> 33.6 us
    ppermute x0 -> x3, waiting for transfers between devices: none -> 219 us  [the longest x2 156 us: collect(): lax.ppermute(going_up, axis, [(d, (d + 1) % ways) for d in range(ways)])]
    reduce_scatter x1, waiting for transfers between devices: 148 us -> 52.9 us  [per_device(): lax.psum_scatter(grads[8].astype(jnp.bfloat16), 'fsdp', scatter_dimension...]
    reduce_scatter x1, waiting for transfers between devices: 19.9 us -> 0.02 us  [per_device(): lax.psum_scatter(grads[2].astype(jnp.bfloat16), 'fsdp', scatter_dimension...]
  transfers between devices with their start and end apart: 10 -> 13, of which waited for: 7 -> 9; matrix products, arithmetic and copies ran while one was open for 26% -> 24% of each run, Pallas kernels for 0% -> 0%
where the time goes in v1:
time: 1270 us; the launch traced here: 1260 us
  waiting for transfers between devices  772 us (61%)
  matrix products  287 us (23%)
  blocking collectives  117 us (9%)
  local copies, waits for them, and re-layouts  33.6 us (3%)
  other arithmetic  31.7 us (2%)
  between operations  16.3 us (1%)
    ppermute x2, waiting for transfers between devices, collect(): lax.ppermute(going_up, axis, [(d, (d + 1) % ways) for d in range(ways)])  156 us
    reduce_scatter x1, waiting for transfers between devices, per_device(): lax.psum_scatter(grads[6].astype(jnp.bfloat16), 'fsdp', scatter_dimension...  146 us
    all_gather x1, waiting for transfers between devices, per_device(): lax.all_gather(w_fc1, 'fsdp', axis=0, tiled=True)  139 us
    all_gather x1, waiting for transfers between devices, per_device(): lax.all_gather(w_fc2, 'fsdp', axis=0, tiled=True)  121 us
    ppermute x1, waiting for transfers between devices, collect(): lax.ppermute(going_down, axis, [(d, (d - 1) % ways) for d in range(ways)])  63.2 us
    reduce_scatter x1, waiting for transfers between devices, per_device(): lax.psum_scatter(grads[8].astype(jnp.bfloat16), 'fsdp', scatter_dimension...  52.9 us
    psum x1, waiting for transfers between devices, per_device(): lax.psum(shares[2].astype(jnp.bfloat16), 'dp').astype(jnp.float32)  50.6 us
    dot_general x16, matrix products, attend(): jnp.einsum('hqk,khd->qhd', probs, value_pair, preferred_element_type=jnp....  41.9 us
  transfers between devices with their start and end apart: 13, of which 9 were waited for; matrix products, arithmetic and copies ran while one was open for 24% of the time, Pallas kernels for 0%

profile of v1, /device:TPU:0, one launch (start us, length us, event | category | flops | bytes accessed | tf_op | source)
XLA Modules:
  0.0 1262.9 jit_solution(16188292871126044453)
XLA Ops:
  10.2 15.1 %all_gather.39 = bf16[50,1024]{1,0:T(8,128)(2,1)S(1)} all-gather(bf16[50,256]{1,0:T(8,128)(2,1)S(1)} %copy-done.18), channel_id=1, replica_groups=mesh['dp'=8,'fsdp'=4] {'fsdp'}, dimensions={1}, use_global_device_ids=true | all-gather | bytes 128000 | tf_op jit(solution)/shard_map/all_gather | solution.py:243
  27.7 12.1 all-gather
  39.8 8.5 all-gather.1
  48.3 14.2 %all-gather.2 = bf16[4,1,256]{2,1,0:T(2,128)(2,1)S(1)} all-gather(bf16[1,1,256]{2,1,0:T(2,128)(2,1)S(1)} %reshape.261), channel_id=1, replica_groups=mesh['dp'=8,'fsdp'=4] {'fsdp'}, dimensions={0}, use_global_device_ids=true | all-gather | bytes 2560 | tf_op jit(solution)/shard_map/all_gather | solution.py:238
  62.5 17.2 %all_gather.47 = bf16[4096]{0:T(1024)(128)(2,1)S(1)} all-gather(bf16[1024]{0:T(1024)(128)(2,1)S(1)} %copy-done.24), channel_id=1, replica_groups=mesh['dp'=8,'fsdp'=4] {'fsdp'}, dimensions={0}, use_global_device_ids=true | all-gather | bytes 10240 | tf_op jit(solution)/shard_map/all_gather | solution.py:241
  79.7 8.2 all-gather.3
  88.0 40.0 %all-gather.9.cloned.1.call-done = bf16[1024,3072]{1,0:T(8,128)(2,1)} async-done(((bf16[256,3072]{1,0:T(8,128)(2,1)}), bf16[1024,3072]{1,0:T(8,128)(2,1)}) %all-gather.9.cloned.1.call-update) | async-done | bytes 6291472 | tf_op jit(solution)/shard_map/all_gather | solution.py:236
  128.0 6.6 convolution_convert_fusion.5
  142.5 36.8 %while.40 = (s32[]{:T(128)}, bf16[8,512,2,64]{1,3,2,0:T(8,128)(2,1)}, f32[8,2,512]{2,1,0:T(2,128)S(1)}, bf16[8,512,2,64]{1,3,2,0:T(8,128)(2,1)}, bf16[8,512,2,64...) while((s32[]{:T(128)}, ...), condition=%wide.region_12.13_spmd.clone, body=%wide.region_9.12_spmd.clone.sunk | while | flops 140835840 | bytes 7901273 | solution.py:101
  179.3 4.0 fusion.218
  184.9 138.7 %all-gather.13.cloned.1.call-done = bf16[1024,4096]{1,0:T(8,128)(2,1)} async-done(((bf16[256,4096]{1,0:T(8,128)(2,1)}), bf16[1024,4096]{1,0:T(8,128)(2,1)}) %all-gather.13.cloned.1.call-update) | async-done | bytes 8388624 | tf_op jit(solution)/shard_map/all_gather | solution.py:240
  323.6 28.0 %fusion.98 = (f32[512,4096]{1,0:T(8,128)}, f32[512,4096]{1,0:T(8,128)}) fusion(f32[4096]{0:T(1024)S(1)} %convert_element_type.184, bf16[1024,4096]{1,0:T(8,128)(2,1)} %all-gather.13.cloned.1.call-done, f32[512,1024]{1,0:T(8,128)} %copy-done.3, f32[512]{0:T(512)S(1)} %fusion.171, f32[512]{0:T(512)S(1)} %broadcast_multiply_fusion, f32[1024]{0:T(1024)S(1)} %bitcast.218, ...), kind=kOutput, calls=%fused_computation.96 | convolution fusion | flops 4429709312 | bytes 27291648 | tf_op jit(solution)/shard_map/dot_general | solution.py:107
  351.6 121.2 %all-gather.15.cloned.1.call-done = bf16[4096,1024]{1,0:T(8,128)(2,1)} async-done(((bf16[1024,1024]{1,0:T(8,128)(2,1)}), bf16[4096,1024]{1,0:T(8,128)(2,1)}) %all-gather.15.cloned.1.call-update) | async-done | bytes 8388624 | tf_op jit(solution)/shard_map/all_gather | solution.py:256
  472.9 15.7 %fusion.219 = (bf16[4096]{0:T(1024)(128)(2,1)}, bf16[512,4096]{1,0:T(8,128)(2,1)}) fusion(f32[512,4096]{1,0:T(8,128)} %get-tuple-element.283, bf16[4096,1024]{1,0:T(8,128)(2,1)} %all-gather.15.cloned.1.call-done, bf16[512,1024]{1,0:T(8,128)(2,1)} %param.21, pred[512]{0:T(512)(128)(4,1)S(1)} %broadcast_select_fusion.1, f32[512,4096]{1,0:T(8,128)} %get-tuple-element.284, ...), kind=kOutput, calls=%fused_computation.283 | convolution fusion | flops 4329041920 | bytes 30433792 | tf_op jit(solution)/shard_map/rd,fd->rf/dot_general | solution.py:142
  488.6 9.3 multiply_reduce_fusion.1
  501.4 2.6 convolution_convert_fusion.6
  504.0 4.2 convolution_convert_fusion.7
  509.9 72.4 %while.41 = (s32[]{:T(128)}, bf16[8,512,2,64]{1,3,2,0:T(8,128)(2,1)}, bf16[8,512,2,64]{1,3,2,0:T(8,128)(2,1)}, bf16[8,512,2,64]{1,3,2,0:T(8,128)(2,1)}, bf16[8,5...) while((s32[]{:T(128)}, ...), condition=%wide.region_19.20_spmd.clone, body=%wide.region_17.19_spmd.clone.sunk | while | flops 340655104 | bytes 17984624 | solution.py:184
  582.3 8.2 convolution_convert_fusion.4
  591.8 15.0 %convolution_convert_fusion.2 = bf16[4096,1024]{1,0:T(8,128)(2,1)} fusion(f32[512,4096]{1,0:T(8,128)} %get-tuple-element.283, f32[512,4096]{1,0:T(8,128)} %get-tuple-element.284, f32[4096]{0:T(1024)S(1)} %convert_element_type.184, bf16[512,1024]{1,0:T(8,128)(2,1)S(1)} %copy-done.7, pred[512]{0:T(512)(128)(4,1)S(1)} %broadcast_select_fusion.1), kind=kOutput, calls=%fused_computation.127 | convolution fusion | flops 4308074496 | bytes 26231296 | tf_op jit(solution)/shard_map/rf,rd->fd/dot_general | solution.py:141
  606.9 10.9 convolution_convert_fusion.3
  617.9 3.8 collective-permute-start.1
  621.7 91.7 %collective-permute-done = bf16[1024,1024]{1,0:T(8,128)(2,1)} collective-permute-done((bf16[1024,1024]{1,0:T(8,128)(2,1)}, bf16[1024,1024]{1,0:T(8,128)(2,1)}, u32[]{:S(2)}, u32[]{:S(2)}) %collective-permute-start) | collective-permute-done | bytes 2097184 | tf_op jit(solution)/shard_map/ppermute | solution.py:21
  715.9 4.3 broadcast_in_dim.136
  721.7 3.1 constant_dynamic-update-slice_fusion.2
  724.8 63.2 %collective-permute-done.1 = bf16[1024,1024]{1,0:T(8,128)(2,1)} collective-permute-done((bf16[1024,1024]{1,0:T(8,128)(2,1)}, bf16[1024,1024]{1,0:T(8,128)(2,1)}, u32[]{:S(2)}, u32[]{:S(2)}) %collective-permute-start.1) | collective-permute-done | bytes 2097184 | tf_op jit(solution)/shard_map/ppermute | solution.py:24
  788.0 3.1 constant_dynamic-update-slice_fusion.1
  791.1 64.5 %collective-permute-done.2 = bf16[1024,1024]{1,0:T(8,128)(2,1)} collective-permute-done((bf16[1024,1024]{1,0:T(8,128)(2,1)}, bf16[1024,1024]{1,0:T(8,128)(2,1)}, u32[]{:S(2)}, u32[]{:S(2)}) %collective-permute-start.2) | collective-permute-done | bytes 2097184 | tf_op jit(solution)/shard_map/ppermute | solution.py:21
  855.6 3.1 constant_dynamic-update-slice_fusion
  859.8 40.7 %while.39 = (s32[]{:T(128)}, bf16[8,512,2,64]{1,3,2,0:T(8,128)(2,1)}, bf16[8,512,2,64]{1,3,2,0:T(8,128)(2,1)}, bf16[8,512,2,64]{1,3,2,0:T(8,128)(2,1)}, bf16[8,5...) while((s32[]{:T(128)}, bf16[8,512,2,64]{1,3,2,0:T(8,128)(2,1)}, ...), condition=%wide.region_6.7_spmd.clone, body=%wide.region_3.6_spmd.clone.sunk | while | flops 206374912 | bytes 1586253 | solution.py:101
  861.9 2.9 fusion.273
  867.0 2.9 fusion.273
  872.1 2.9 fusion.273
  877.2 2.9 fusion.273
  882.3 2.9 fusion.273
  887.3 2.9 fusion.273
  892.4 2.9 fusion.273
  897.5 3.0 fusion.273
  900.5 3.4 fusion.217
  905.6 7.3 multiply_reduce_fusion.2
  918.2 52.9 %reduce-scatter.12.cloned.1.call-done = bf16[1024,1024]{1,0:T(8,128)(2,1)} async-done(((bf16[4096,1024]{1,0:T(8,128)(2,1)}), bf16[1024,1024]{1,0:T(8,128)(2,1)}) %reduce-scatter.12.cloned.1.call-update) | async-done | bytes 2097168 | tf_op jit(solution)/shard_map/reduce_scatter | solution.py:287
  971.1 146.1 %reduce-scatter.10.cloned.1.call-done = bf16[256,4096]{1,0:T(8,128)(2,1)} async-done(((bf16[1024,4096]{1,0:T(8,128)(2,1)}), bf16[256,4096]{1,0:T(8,128)(2,1)}) %reduce-scatter.10.cloned.1.call-update) | async-done | bytes 2097168 | tf_op jit(solution)/shard_map/reduce_scatter | solution.py:281
  1117.2 32.4 %select_convert_fusion = bf16[512,1024]{1,0:T(8,128)(2,1)} fusion(f32[512,1024]{1,0:T(8,128)S(1)} %copy-done.10, bf16[4096,1024]{1,0:T(8,128)(2,1)} %constant_dynamic-update-slice_fusion, bf16[1024,4096]{1,0:T(8,128)(2,1)} %all-gather.13.cloned.1.call-done, f32[4096]{0:T(1024)S(1)} %convert_element_type.184, f32[1024]{0:T(1024)S(1)} %bitcast.220, ...), kind=kOutput, calls=%fused_computation.176 | convolution fusion | flops 8732540928 | bytes 19952128 | tf_op jit(solution)/shard_map/dot_general | solution.py:111
  1149.7 18.1 %all-reduce.7 = (bf16[1024]{0:T(1024)(128)(2,1)S(1)}, bf16[1024]{0:T(1024)(128)(2,1)S(1)}, bf16[1024]{0:T(1024)(128)(2,1)S(1)}, bf16[1024]{0:T(1024)(128)(2,1)S(1)}, bf16[4096]{0:T(1024)(128)(2,1)S(1)}) all-reduce(bf16[1024]{0:T(1024)(128)(2,1)S(1)} %get-tuple-element.199, ...), channel_id=2, replica_groups=mesh['dp'=8,'fsdp'=4] {'fsdp'}, use_global_device_ids=true, to_apply=%region_23.24.clone | all-reduce | flops 8192 | bytes 32768
  1168.1 23.9 %all-reduce.5 = (bf16[256]{0:T(256)(128)(2,1)S(1)}, bf16[256]{0:T(256)(128)(2,1)S(1)}, bf16[256]{0:T(256)(128)(2,1)S(1)}, bf16[256]{0:T(256)(128)(2,1)S(1)}, bf1...) all-reduce(bf16[256]{0:T(256)(128)(2,1)S(1)} %dynamic-slice.1, ...), channel_id=1, replica_groups=mesh['dp'=8,'fsdp'=4] {'dp'}, use_global_device_ids=true, to_apply=%region_24.25 | all-reduce | flops 14848 | bytes 59392 | tf_op jit(solution)/shard_map/psum | solution.py:295
  1195.5 50.6 %all-reduce.10.cloned.1.call-done = (bf16[256,3072]{1,0:T(8,128)(2,1)}, bf16[256,1024]{1,0:T(8,128)(2,1)}, bf16[256,4096]{1,0:T(8,128)(2,1)}, bf16[1024,1024]{1,0:T(8,128)(2,1)}) async-done(((bf16[256,3072]{1,0:T(8,128)(2,1)}, bf16[256,1024]{1,0:T(8,128)(2,1)}, bf16[256,4096]{1,0:T(8,128)(2,1)}, bf16[1024,1024]{1,0:T(8,128)(2,1)}), (bf16[256,3072]{1,0:T(8,128)(2,1)}, bf16[256,1024]{1,0:T(8,128)(2,1)}, ...) | async-done | bytes 6291472 | tf_op jit(solution)/shard_map/psum | solution.py:297
  1246.0 4.2 convert_element_type.206
  1250.3 2.5 convert_element_type.210
  (274 shorter events, 164.8 us)
Async XLA Ops:
  7.2 3.0 copy-start.18
  7.2 18.2 %copy-start.23 = (s32[145,4]{0,1:T(4,128)S(1)}, s32[145,4]{0,1:T(4,128)}, u32[]{:S(2)}) copy-start(s32[145,4]{0,1:T(4,128)} %param.32) | copy-start | bytes 6964
  7.2 18.1 %copy-start.22 = (f32[145,4]{0,1:T(4,128)S(1)}, f32[145,4]{0,1:T(4,128)}, u32[]{:S(2)}) copy-start(f32[145,4]{0,1:T(4,128)} %param.33) | copy-start | bytes 6964
  7.2 18.8 %copy-start.12 = (bf16[512,1024]{1,0:T(8,128)(2,1)S(1)}, bf16[512,1024]{1,0:T(8,128)(2,1)}, u32[]{:S(2)}) copy-start(bf16[512,1024]{1,0:T(8,128)(2,1)} %param.20) | copy-start | bytes 3145732
  7.2 20.4 %copy-start.29 = (bf16[256]{0:T(256)(128)(2,1)S(1)}, bf16[256]{0:T(256)(128)(2,1)}, u32[]{:S(2)}) copy-start(bf16[256]{0:T(256)(128)(2,1)} %param.22) | copy-start | bytes 1540
  7.2 32.6 %copy-start.30 = (bf16[256]{0:T(256)(128)(2,1)S(1)}, bf16[256]{0:T(256)(128)(2,1)}, u32[]{:S(2)}) copy-start(bf16[256]{0:T(256)(128)(2,1)} %param.23) | copy-start | bytes 1540
  7.2 41.0 %copy-start.31 = (bf16[256]{0:T(256)(128)(2,1)S(1)}, bf16[256]{0:T(256)(128)(2,1)}, u32[]{:S(2)}) copy-start(bf16[256]{0:T(256)(128)(2,1)} %param.26) | copy-start | bytes 1540
  7.3 55.2 %copy-start.24 = (bf16[1024]{0:T(1024)(128)(2,1)S(1)}, bf16[1024]{0:T(1024)(128)(2,1)}, u32[]{:S(2)}) copy-start(bf16[1024]{0:T(1024)(128)(2,1)} %param.29) | copy-start | bytes 6148
  7.3 72.5 %copy-start.32 = (bf16[256]{0:T(256)(128)(2,1)S(1)}, bf16[256]{0:T(256)(128)(2,1)}, u32[]{:S(2)}) copy-start(bf16[256]{0:T(256)(128)(2,1)} %param.27) | copy-start | bytes 1540
  7.3 120.7 %all-gather.9.cloned.1.call-start = ((), (), s32[]{:S(2)}) async-start(), calls=%async_computation.5 | async-start | bytes 7864320 | tf_op jit(solution)/shard_map/all_gather | solution.py:236
  8.0 171.3 %all-gather.11.cloned.1.call-start = ((), (), s32[]{:S(2)}) async-start(), calls=%async_computation.6 | async-start | bytes 2621440 | tf_op jit(solution)/shard_map/all_gather | solution.py:237
  8.8 314.9 %all-gather.13.cloned.1.call-start = ((), (), s32[]{:S(2)}) async-start(), calls=%async_computation.7 | async-start | bytes 10485760 | tf_op jit(solution)/shard_map/all_gather | solution.py:240
  9.5 463.4 %all-gather.15.cloned.1.call-start = ((), (), s32[]{:S(2)}) async-start(), calls=%async_computation.8 | async-start | bytes 10485760 | tf_op jit(solution)/shard_map/all_gather | solution.py:256
  10.1 908.1 %reduce-scatter.8.cloned.1.call-start = ((), (), s32[]{:S(2)}) async-start(), calls=%async_computation.10 | async-start | bytes 2621440 | tf_op jit(solution)/shard_map/reduce_scatter | solution.py:272
  26.0 108.6 %copy-start.16 = (f32[512,50]{0,1:T(8,128)}, f32[512,50]{0,1:T(8,128)S(1)}, u32[]{:S(2)}) copy-start(f32[512,50]{0,1:T(8,128)S(1)} %convolution_select_fusion) | copy-start | bytes 307204
  27.6 34.9 %copy-start.19 = (f32[512]{0:T(512)}, f32[512]{0:T(512)S(1)}, u32[]{:S(2)}) copy-start(f32[512]{0:T(512)S(1)} %multiply_reduce_fusion.7) | copy-start | bytes 6148
  179.3 172.4 %copy-start.5 = (bf16[8,512,2,64]{1,3,2,0:T(8,128)(2,1)}, bf16[8,512,2,64]{1,3,2,0:T(8,128)(2,1)S(1)}, u32[]{:S(2)}) copy-start(bf16[8,512,2,64]{1,3,2,0:T(8,128)(2,1)S(1)} %get-tuple-element.547) | copy-start | bytes 3145732
  183.2 1.3 copy-start.3
  472.9 15.7 %copy-start.4 = (f32[512,1024]{1,0:T(8,128)S(1)}, f32[512,1024]{1,0:T(8,128)}, u32[]{:S(2)}) copy-start(f32[512,1024]{1,0:T(8,128)} %copy-done.3) | copy-start | bytes 6291460
  497.9 2.1 copy-start.6
  497.9 3.4 copy-start.13
  498.6 1.3 copy-start
  500.4 1.0 copy-start.14
  504.0 414.2 %reduce-scatter.6.cloned.1.call-start = ((), (), s32[]{:S(2)}) async-start(), calls=%async_computation.9 | async-start | bytes 7864320 | tf_op jit(solution)/shard_map/reduce_scatter | solution.py:269
  590.6 1.2 copy-start.7
  590.6 380.5 %reduce-scatter.12.cloned.1.call-start = ((), (), s32[]{:S(2)}) async-start(), calls=%async_computation.12 | async-start | bytes 10485760 | tf_op jit(solution)/shard_map/reduce_scatter | solution.py:287
  606.8 510.3 %reduce-scatter.10.cloned.1.call-start = ((), (), s32[]{:S(2)}) async-start(), calls=%async_computation.11 | async-start | bytes 10485760 | tf_op jit(solution)/shard_map/reduce_scatter | solution.py:281
  617.8 96.2 %copy-start.33 = (u32[32]{0:T(128)S(1)}, u32[32]{0:T(128)}, u32[]{:S(2)}) copy-start(u32[32]{0:T(128)} %constant.226) | copy-start | bytes 388
  617.8 550.3 %reduce-scatter.14.cloned.1.call-start = ((), (), s32[]{:S(2)}) async-start(), calls=%async_computation.13 | async-start | bytes 143360 | tf_op jit(solution)/shard_map/reduce_scatter | solution.py:290
  617.8 95.6 %collective-permute-start = (bf16[1024,1024]{1,0:T(8,128)(2,1)}, bf16[1024,1024]{1,0:T(8,128)(2,1)}, u32[]{:S(2)}, u32[]{:S(2)}) collective-permute-start(bf16[1024,1024]{1,0:T(8,128)(2,1)} %param.30), channel_id=1, source_target_pairs={{0,1},{1,2},{2,3},{3,0},{4,5},{5,6},{6,7},{7,4},{8,9},{9,10},{10,1... | collective-permute-start | bytes 6291464 | tf_op jit(solution)/shard_map/ppermute | solution.py:21
  617.9 170.1 %collective-permute-start.1 = (bf16[1024,1024]{1,0:T(8,128)(2,1)}, bf16[1024,1024]{1,0:T(8,128)(2,1)}, u32[]{:S(2)}, u32[]{:S(2)}) collective-permute-start(bf16[1024,1024]{1,0:T(8,128)(2,1)} %param.30), channel_id=1, source_target_pairs={{0,3},{1,0},{2,1},{3,2},{4,7},{5,4},{6,5},{7,6},{8,11},{9,8},{10,9... | collective-permute-start | bytes 6291464 | tf_op jit(solution)/shard_map/ppermute | solution.py:24
  713.4 142.1 %collective-permute-start.2 = (bf16[1024,1024]{1,0:T(8,128)(2,1)}, bf16[1024,1024]{1,0:T(8,128)(2,1)}, u32[]{:S(2)}, u32[]{:S(2)}) collective-permute-start(bf16[1024,1024]{1,0:T(8,128)(2,1)} %collective-permute-done), channel_id=1, source_target_pairs={{0,1},{1,2},{2,3},{3,0},{4,5},{5,6},{6,7},{7,4},{8,9},{9,10},{10,1... | collective-permute-start | bytes 6291464 | tf_op jit(solution)/shard_map/ppermute | solution.py:21
  715.9 4.3 copy-start.2
  900.5 5.1 copy-start.27
  900.5 5.1 copy-start.28
  903.9 1.3 copy-start.9
  905.6 7.3 copy-start.20
  912.9 1.6 copy-start.1
  912.9 3.1 copy-start.17
  916.0 201.2 %copy-start.10 = (f32[512,1024]{1,0:T(8,128)S(1)}, f32[512,1024]{1,0:T(8,128)}, u32[]{:S(2)}) copy-start(f32[512,1024]{1,0:T(8,128)} %copy-done.9) | copy-start | bytes 6291460
  918.0 328.0 %all-reduce.10.cloned.1.call-start = ((), (), s32[]{:S(2)}) async-start(), calls=%async_computation.14 | async-start | bytes 12582912 | tf_op jit(solution)/shard_map/psum | solution.py:297
  1117.2 32.5 %copy-start.21 = (bf16[4096]{0:T(1024)(128)(2,1)S(1)}, bf16[4096]{0:T(1024)(128)(2,1)}, u32[]{:S(2)}) copy-start(bf16[4096]{0:T(1024)(128)(2,1)} %get-tuple-element.287) | copy-start | bytes 24580
  1117.2 32.5 %copy-start.25 = (bf16[1024]{0:T(1024)(128)(2,1)S(1)}, bf16[1024]{0:T(1024)(128)(2,1)}, u32[]{:S(2)}) copy-start(bf16[1024]{0:T(1024)(128)(2,1)} %get-tuple-element.197) | copy-start | bytes 6148
  1117.2 32.4 %copy-start.26 = (bf16[1024]{0:T(1024)(128)(2,1)S(1)}, bf16[1024]{0:T(1024)(128)(2,1)}, u32[]{:S(2)}) copy-start(bf16[1024]{0:T(1024)(128)(2,1)} %get-tuple-element.201) | copy-start | bytes 6148
  1246.0 4.3 copy-start.8
  1246.0 6.7 copy-start.11
  1250.3 4.5 copy-start.15
Sparse Core Ops, SparseCore 0:
  9.7 118.3 all-gather.8
  129.6 43.9 all-gather.10
  175.1 148.4 all-gather.12
  325.0 147.7 all-gather.14
  504.1 41.8 reduce-scatter.7
  590.7 193.2 reduce-scatter.5
  786.4 184.6 reduce-scatter.11
  973.4 143.6 reduce-scatter.9
  1120.0 20.0 reduce-scatter.13
  1143.5 102.4 all-reduce.9
